TPU v7x, 256 devices: a whole 4x4x8 slice. The times are simulated.
256 devices in a mesh: dp: 4 (over y), expert: 16 (over z, core), ffn: 4 (over x).
Axes of the slice: x: 4, y: 4, z: 8, core: 2. Of those that a mesh axis runs over, the one named last changes fastest.
Arguments:
- tokens: bfloat16 [8192, 7168], P(('dp', 'expert'), 'ffn'), may hold values from -6 to 6
- grad_out: bfloat16 [8192, 7168], P(('dp', 'expert'), 'ffn'), may hold values from -3 to 3
- route_ids: int32 [8192, 2], P(('dp', 'expert')), may hold values from 0 to 15, all different within a row; in each aligned block of 128 rows (0 to 127, 128 to 255, ...) at most 20 rows name the same one
- combine: float32 [8192, 2], P(('dp', 'expert')), may hold values from 0.2 to 1
- gate_weight: bfloat16 [16, 7168, 1024], P('expert', 'dp', 'ffn'), may hold values from -0.0625 to 0.0625
- up_weight: bfloat16 [16, 7168, 1024], P('expert', 'dp', 'ffn'), may hold values from -0.0625 to 0.0625
- down_weight: bfloat16 [16, 1024, 7168], P('expert', 'ffn', 'dp'), may hold values from -0.1875 to 0.1875
Outputs:
- grad_tokens: bfloat16 [8192, 7168], P(('dp', 'expert'), 'ffn')
- grad_gate: float32 [16, 7168, 1024], P('expert', 'dp', 'ffn')
- grad_up: float32 [16, 7168, 1024], P('expert', 'dp', 'ffn')
- grad_down: float32 [16, 1024, 7168], P('expert', 'ffn', 'dp')
Inputs may be any that keep to these rules, and one draw needn't show every extreme that they name: `route_ids`: each row names 2 different experts; every expert is named by some row. In each aligned block of 128 rows (the rows of one device) no expert is named by more than 20 rows, a bound that some block reaches.
All inputs are finite; a program needn't handle non-finite values.
Results may differ from a plain program's by a relative error of at most 0.019.
Values may be sent and summed in bfloat16 or wider, within the bound.
No kernel may reach another device: no remote copies, remote signals or barrier semaphores. Data moves between devices by JAX's collectives and lax.ppermute only.
A program may use at most 128 MiB of HBM per device.

v0:
```python
import jax
import jax.numpy as jnp
from jax import lax
from jax.sharding import PartitionSpec as P


def activations(gate, up, grad_hidden):
    sig = jax.nn.sigmoid(gate)
    hidden = (gate * sig * up).astype(jnp.bfloat16)
    grad_up_act = (grad_hidden * gate * sig).astype(jnp.bfloat16)
    grad_gate_act = (grad_hidden * up * sig * (1.0 + gate * (1.0 - sig))).astype(jnp.bfloat16)
    return (hidden, grad_up_act, grad_gate_act)


def per_device(tokens, grad_out, route_ids, combine, gate_weight, up_weight, down_weight):
    tok_rows = tokens.shape[0]
    top = route_ids.shape[1]
    groups = lax.axis_size("expert")
    experts = gate_weight.shape[0] * groups
    capacity = min(tok_rows, (5 * top * tok_rows + 4 * experts - 1) // (4 * experts))
    slot_count = tok_rows * top
    expert_of = route_ids.reshape(slot_count)
    onehot = (expert_of[:, None] == jnp.arange(experts, dtype=jnp.int32)[None, :]).astype(jnp.int32)
    earlier = jnp.cumsum(onehot, axis=0) - onehot
    position = jnp.sum(earlier * onehot, axis=1)
    target = expert_of * capacity + position
    placing = (jnp.arange(experts * capacity, dtype=jnp.int32)[:, None] == target[None, :]).astype(
        jnp.bfloat16
    )
    placing_tok = jnp.sum(placing.reshape(experts * capacity, tok_rows, top), axis=2)
    scaled = (combine[:, :, None] * grad_out[:, None, :].astype(jnp.float32)).astype(jnp.bfloat16)
    scaled = scaled.reshape(slot_count, grad_out.shape[1])

    def pack(matrix, rows):
        packed = jnp.dot(matrix, rows, preferred_element_type=jnp.float32).astype(jnp.bfloat16)
        return packed.reshape(groups, capacity, rows.shape[1])

    full_tok, full_z = (
        lax.all_gather(tokens, "ffn", axis=1, tiled=True),
        lax.all_gather(scaled, "ffn", axis=1, tiled=True),
    )
    recv_x, recv_z = (
        lax.all_to_all(
            pack(placing_tok, full_tok), "expert", split_axis=0, concat_axis=0, tiled=True
        ),
        lax.all_to_all(pack(placing, full_z), "expert", split_axis=0, concat_axis=0, tiled=True),
    )
    width = recv_x.shape[2]
    row_count = groups * capacity
    x_rows = recv_x.reshape(row_count, width)
    z_rows = recv_z.reshape(row_count, width)
    over_rows = (((0,), (0,)), ((), ()))
    over_units = (((1,), (1,)), ((), ()))
    gathered_w = (
        lax.all_gather(gate_weight, "dp", axis=1, tiled=True),
        lax.all_gather(up_weight, "dp", axis=1, tiled=True),
        lax.all_gather(down_weight, "dp", axis=2, tiled=True),
    )
    w_gate = gathered_w[0][0]
    w_up = gathered_w[1][0]
    w_down = gathered_w[2][0]
    gate = jnp.dot(x_rows, w_gate, preferred_element_type=jnp.float32)
    up = jnp.dot(x_rows, w_up, preferred_element_type=jnp.float32)
    grad_hidden = lax.dot_general(z_rows, w_down, over_units, preferred_element_type=jnp.float32)
    hidden, grad_up_act, grad_gate_act = activations(gate, up, grad_hidden)
    part_gate = lax.dot_general(
        x_rows, grad_gate_act, over_rows, preferred_element_type=jnp.float32
    )
    part_up = lax.dot_general(x_rows, grad_up_act, over_rows, preferred_element_type=jnp.float32)
    part_down = lax.dot_general(hidden, z_rows, over_rows, preferred_element_type=jnp.float32)
    grad_gate, grad_up, grad_down = (
        lax.psum_scatter(
            part_gate[None].astype(jnp.bfloat16), "dp", scatter_dimension=1, tiled=True
        ).astype(jnp.float32),
        lax.psum_scatter(
            part_up[None].astype(jnp.bfloat16), "dp", scatter_dimension=1, tiled=True
        ).astype(jnp.float32),
        lax.psum_scatter(
            part_down[None].astype(jnp.bfloat16), "dp", scatter_dimension=2, tiled=True
        ).astype(jnp.float32),
    )
    slot_partial = lax.dot_general(
        grad_gate_act, w_gate, over_units, preferred_element_type=jnp.float32
    )
    slot_partial = slot_partial + lax.dot_general(
        grad_up_act, w_up, over_units, preferred_element_type=jnp.float32
    )
    summed = lax.psum_scatter(
        slot_partial.astype(jnp.bfloat16), "ffn", scatter_dimension=1, tiled=True
    )
    piece = summed.shape[1]
    returned = lax.all_to_all(
        summed.reshape(groups, capacity, piece), "expert", split_axis=0, concat_axis=0, tiled=True
    )
    slot_grad = returned.reshape(experts * capacity, piece)
    per_slot = lax.dot_general(placing, slot_grad, over_rows, preferred_element_type=jnp.float32)
    grad_tokens = jnp.sum(per_slot.reshape(tok_rows, top, slot_grad.shape[1]), axis=1).astype(
        jnp.bfloat16
    )
    return (grad_tokens, grad_gate, grad_up, grad_down)


def solution(mesh):
    return jax.shard_map(
        per_device,
        mesh=mesh,
        in_specs=(
            P(("dp", "expert"), "ffn"),
            P(("dp", "expert"), "ffn"),
            P(("dp", "expert"), None),
            P(("dp", "expert"), None),
            P("expert", "dp", "ffn"),
            P("expert", "dp", "ffn"),
            P("expert", "ffn", "dp"),
        ),
        out_specs=(
            P(("dp", "expert"), "ffn"),
            P("expert", "dp", "ffn"),
            P("expert", "dp", "ffn"),
            P("expert", "ffn", "dp"),
        ),
        check_vma=False,
    )
```

profile of v0, /device:TPU:1, one launch (start us, length us, event | category | flops | bytes accessed | tf_op | source)
XLA Modules:
  0.0 535.1 jit_solution(14944798309835122971)
XLA Ops:
  7.2 0.7 all-gather.10.cloned.1.call-update
  7.9 0.8 copy.30
  8.7 0.1 mul.63
  8.9 2.7 mul.65
  11.6 2.6 mul.66
  14.2 1.1 multiply_convert_fusion
  15.4 0.1 reshape.100
  15.5 0.1 eq.62
  15.7 0.6 reduce-window.6
  16.3 0.2 slice_reduce_fusion
  16.6 0.1 reduce_sum.33
  16.9 27.7 %all-gather.10.cloned.1.call-done = bf16[128,7168]{1,0:T(8,128)(2,1)} async-done(((bf16[128,1792]{1,0:T(8,128)(2,1)}), bf16[128,7168]{1,0:T(8,128)(2,1)}) %all-gather.10.cloned.1.call-update) | async-done | bytes 1835024 | tf_op jit(solution)/shard_map/all_gather | solution.py:39
  44.6 4.9 convolution_convert_fusion
  49.5 7.3 %reshape.104 = bf16[16,20,7168]{2,1,0:T(8,128)(2,1)} reshape(bf16[320,7168]{1,0:T(8,128)(2,1)} %convolution_convert_fusion) | data formatting | bytes 9175040 | tf_op jit(solution)/shard_map/reshape | solution.py:36
  56.8 7.9 %all-to-all-start.1 = ((bf16[16,20,7168]{2,1,0:T(8,128)(2,1)}), bf16[16,20,7168]{2,1,0:T(8,128)(2,1)}, u32[]{:S(2)}, u32[]{:S(2)}) async-start(bf16[16,20,7168]{2,1,0:T(8,128)(2,1)} %reshape.104), calls=%async_computation.1 | async-start | bytes 11010048 | tf_op jit(solution)/shard_map/all_to_all | solution.py:43
  64.7 0.7 all-gather.14.cloned.1.call-update
  65.5 0.5 all-gather.12.cloned.1.call-update
  66.0 27.3 %all-gather.6.cloned.1.call-done = bf16[256,7168]{1,0:T(8,128)(2,1)} async-done(((bf16[256,1792]{1,0:T(8,128)(2,1)}), bf16[256,7168]{1,0:T(8,128)(2,1)}) %all-gather.6.cloned.1.call-update) | async-done | bytes 3670032 | tf_op jit(solution)/shard_map/all_gather | solution.py:40
  93.4 5.5 %convolution_convert_fusion.1 = bf16[320,7168]{1,0:T(8,128)(2,1)} fusion(bf16[256,7168]{1,0:T(8,128)(2,1)} %all-gather.6.cloned.1.call-done, s32[256]{0:T(256)S(1)} %multiply_add_fusion.1), kind=kOutput, calls=%fused_computation.2 | convolution fusion | flops 1176780800 | bytes 8258560 | tf_op jit(solution)/shard_map/dot_general | solution.py:35
  98.8 7.3 %reshape.102 = bf16[16,20,7168]{2,1,0:T(8,128)(2,1)} reshape(bf16[320,7168]{1,0:T(8,128)(2,1)} %convolution_convert_fusion.1) | data formatting | bytes 9175040 | tf_op jit(solution)/shard_map/reshape | solution.py:36
  106.1 80.2 %all-to-all-done.1 = bf16[16,20,7168]{2,1,0:T(8,128)(2,1)} async-done(((bf16[16,20,7168]{2,1,0:T(8,128)(2,1)}), bf16[16,20,7168]{2,1,0:T(8,128)(2,1)}, u32[]{:S(2)}, u32[]{:S(2)}) %all-to-all-start.1) | async-done | bytes 4587552 | tf_op jit(solution)/shard_map/all_to_all | solution.py:43
  186.3 5.5 %all-to-all-start = ((bf16[16,20,7168]{2,1,0:T(8,128)(2,1)}), bf16[16,20,7168]{2,1,0:T(8,128)(2,1)}, u32[]{:S(2)}, u32[]{:S(2)}) async-start(bf16[16,20,7168]{2,1,0:T(8,128)(2,1)} %reshape.102), calls=%async_computation | async-start | bytes 11010048 | tf_op jit(solution)/shard_map/all_to_all | solution.py:46
  191.8 0.5 all-gather.8.cloned.1.call-update
  192.4 0.2 reduce-scatter.5.cloned.1.call-start
  192.6 7.3 %reshape.105 = bf16[320,7168]{1,0:T(8,128)(2,1)} reshape(bf16[16,20,7168]{2,1,0:T(8,128)(2,1)} %all-to-all-done.1) | data formatting | bytes 9175040 | tf_op jit(solution)/shard_map/reshape | solution.py:50
  200.0 4.8 fusion.6
  204.8 5.4 %fusion.9 = f32[320,256]{1,0:T(8,128)S(1)} fusion(bf16[320,7168]{1,0:T(8,128)(2,1)} %reshape.105, bf16[1,7168,256]{2,1,0:T(8,128)(2,1)} %all-gather.12.cloned.1.call-done), kind=kOutput, calls=%fused_computation.15 | convolution fusion | flops 1174405120 | bytes 8585216 | tf_op jit(solution)/shard_map/dot_general | solution.py:63
  210.2 103.2 %all-to-all-done = bf16[16,20,7168]{2,1,0:T(8,128)(2,1)} async-done(((bf16[16,20,7168]{2,1,0:T(8,128)(2,1)}), bf16[16,20,7168]{2,1,0:T(8,128)(2,1)}, u32[]{:S(2)}, u32[]{:S(2)}) %all-to-all-start) | async-done | bytes 4587552 | tf_op jit(solution)/shard_map/all_to_all | solution.py:46
  313.4 7.3 %reshape.103 = bf16[320,7168]{1,0:T(8,128)(2,1)} reshape(bf16[16,20,7168]{2,1,0:T(8,128)(2,1)} %all-to-all-done) | data formatting | bytes 9175040 | tf_op jit(solution)/shard_map/reshape | solution.py:51
  320.8 5.0 multiply_convert_fusion.2
  325.7 1.4 fusion.4
  327.1 0.6 copy-done.1
  327.8 3.6 fusion
  331.4 6.2 %fusion.3 = bf16[1,256,7168]{2,1,0:T(8,128)(2,1)} fusion(bf16[320,7168]{1,0:T(8,128)(2,1)} %reshape.103, f32[320,256]{1,0:T(8,128)S(1)} %fusion.9, f32[320,256]{1,0:T(8,128)S(1)} %fusion.6), kind=kOutput, calls=%fused_computation.9 | convolution fusion | flops 1176731648 | bytes 8912896 | tf_op jit(solution)/shard_map/dot_general | solution.py:70
  337.7 6.3 %fusion.2 = bf16[1,7168,256]{2,1,0:T(8,128)(2,1)} fusion(bf16[320,7168]{1,0:T(8,128)(2,1)} %reshape.105, bf16[320,256]{1,0:T(8,128)(2,1)S(1)} %get-tuple-element.4), kind=kOutput, calls=%fused_computation.8 | convolution fusion | flops 1176240128 | bytes 8421376 | tf_op jit(solution)/shard_map/dot_general | solution.py:69
  344.0 0.3 reduce-scatter.7.cloned.1.call-start
  344.3 6.3 %fusion.1 = bf16[1,7168,256]{2,1,0:T(8,128)(2,1)} fusion(bf16[320,7168]{1,0:T(8,128)(2,1)} %reshape.105, bf16[320,256]{1,0:T(8,128)(2,1)S(1)} %get-tuple-element.5), kind=kOutput, calls=%fused_computation.7 | convolution fusion | flops 1176240128 | bytes 8421376 | tf_op jit(solution)/shard_map/dot_general | solution.py:66
  350.6 31.3 %reduce-scatter.5.cloned.1.call-done = bf16[320,1792]{1,0:T(8,128)(2,1)} async-done(((bf16[320,7168]{1,0:T(8,128)(2,1)}), bf16[320,1792]{1,0:T(8,128)(2,1)}) %reduce-scatter.5.cloned.1.call-update) | async-done | bytes 1146896 | tf_op jit(solution)/shard_map/reduce_scatter | solution.py:88
  381.9 2.3 reshape.106
  384.2 7.8 %all-to-all-start.2 = ((bf16[16,20,1792]{2,1,0:T(8,128)(2,1)}), bf16[16,20,1792]{2,1,0:T(8,128)(2,1)S(1)}, u32[]{:S(2)}, u32[]{:S(2)}) async-start(bf16[16,20,1792]{2,1,0:T(8,128)(2,1)} %reshape.106), calls=%async_computation.3 | async-start | bytes 2752512 | tf_op jit(solution)/shard_map/all_to_all | solution.py:92
  392.2 37.2 %reduce-scatter.11.cloned.1.call-done = bf16[1,256,1792]{2,1,0:T(8,128)(2,1)} async-done(((bf16[1,256,7168]{2,1,0:T(8,128)(2,1)}), bf16[1,256,1792]{2,1,0:T(8,128)(2,1)}) %reduce-scatter.11.cloned.1.call-update) | async-done | bytes 917520 | tf_op jit(solution)/shard_map/reduce_scatter | solution.py:78
  429.3 2.5 convert_element_type.89
  431.9 44.9 %reduce-scatter.9.cloned.1.call-done = bf16[1,1792,256]{2,1,0:T(8,128)(2,1)} async-done(((bf16[1,7168,256]{2,1,0:T(8,128)(2,1)}), bf16[1,1792,256]{2,1,0:T(8,128)(2,1)}) %reduce-scatter.9.cloned.1.call-update) | async-done | bytes 917520 | tf_op jit(solution)/shard_map/reduce_scatter | solution.py:75
  476.8 2.5 convert_element_type.85
  479.4 44.9 %reduce-scatter.7.cloned.1.call-done = bf16[1,1792,256]{2,1,0:T(8,128)(2,1)} async-done(((bf16[1,7168,256]{2,1,0:T(8,128)(2,1)}), bf16[1,1792,256]{2,1,0:T(8,128)(2,1)}) %reduce-scatter.7.cloned.1.call-update) | async-done | bytes 917520 | tf_op jit(solution)/shard_map/reduce_scatter | solution.py:72
  524.3 2.5 convert_element_type.82
  526.8 0.3 reshape.108
  527.1 1.4 convolution_reduce_fusion
  (32 shorter events, 1.0 us)
Async XLA Ops:
  7.2 37.4 %all-gather.10.cloned.1.call-start = ((), (), s32[]{:S(2)}) async-start(), calls=%async_computation.9 | async-start | bytes 2293760 | tf_op jit(solution)/shard_map/all_gather | solution.py:39
  7.9 85.5 %all-gather.6.cloned.1.call-start = ((), (), s32[]{:S(2)}) async-start(), calls=%async_computation.7 | async-start | bytes 4587520 | tf_op jit(solution)/shard_map/all_gather | solution.py:40
  11.6 3.7 copy-start.2
  56.8 129.5 %all-to-all-start.1 = ((bf16[16,20,7168]{2,1,0:T(8,128)(2,1)}), bf16[16,20,7168]{2,1,0:T(8,128)(2,1)}, u32[]{:S(2)}, u32[]{:S(2)}) async-start(bf16[16,20,7168]{2,1,0:T(8,128)(2,1)} %reshape.104), calls=%async_computation.1 | async-start | bytes 11010048 | tf_op jit(solution)/shard_map/all_to_all | solution.py:43
  64.7 135.3 %all-gather.14.cloned.1.call-start = ((), (), s32[]{:S(2)}) async-start(), calls=%async_computation.11 | async-start | bytes 4587520 | tf_op jit(solution)/shard_map/all_gather | solution.py:55
  65.4 139.3 %all-gather.12.cloned.1.call-start = ((), (), s32[]{:S(2)}) async-start(), calls=%async_computation.10 | async-start | bytes 4587520 | tf_op jit(solution)/shard_map/all_gather | solution.py:56
  186.3 127.1 %all-to-all-start = ((bf16[16,20,7168]{2,1,0:T(8,128)(2,1)}), bf16[16,20,7168]{2,1,0:T(8,128)(2,1)}, u32[]{:S(2)}, u32[]{:S(2)}) async-start(bf16[16,20,7168]{2,1,0:T(8,128)(2,1)} %reshape.102), calls=%async_computation | async-start | bytes 11010048 | tf_op jit(solution)/shard_map/all_to_all | solution.py:46
  191.8 128.9 %all-gather.8.cloned.1.call-start = ((), (), s32[]{:S(2)}) async-start(), calls=%async_computation.8 | async-start | bytes 4587520 | tf_op jit(solution)/shard_map/all_gather | solution.py:57
  192.4 189.5 %reduce-scatter.5.cloned.1.call-start = ((), (), s32[]{:S(2)}) async-start(), calls=%async_computation.12 | async-start | bytes 5734400 | tf_op jit(solution)/shard_map/reduce_scatter | solution.py:88
  320.8 5.0 copy-start
  325.7 2.0 copy-start.1
  331.4 98.0 %reduce-scatter.11.cloned.1.call-start = ((), (), s32[]{:S(2)}) async-start(), calls=%async_computation.15 | async-start | bytes 4587520 | tf_op jit(solution)/shard_map/reduce_scatter | solution.py:78
  337.7 139.1 %reduce-scatter.9.cloned.1.call-start = ((), (), s32[]{:S(2)}) async-start(), calls=%async_computation.14 | async-start | bytes 4587520 | tf_op jit(solution)/shard_map/reduce_scatter | solution.py:75
  344.0 180.3 %reduce-scatter.7.cloned.1.call-start = ((), (), s32[]{:S(2)}) async-start(), calls=%async_computation.13 | async-start | bytes 4587520 | tf_op jit(solution)/shard_map/reduce_scatter | solution.py:72
  384.2 142.7 %all-to-all-start.2 = ((bf16[16,20,1792]{2,1,0:T(8,128)(2,1)}), bf16[16,20,1792]{2,1,0:T(8,128)(2,1)S(1)}, u32[]{:S(2)}, u32[]{:S(2)}) async-start(bf16[16,20,1792]{2,1,0:T(8,128)(2,1)} %reshape.106), calls=%async_computation.3 | async-start | bytes 2752512 | tf_op jit(solution)/shard_map/all_to_all | solution.py:92
Sparse Core Ops, SparseCore 0:
  9.8 34.7 all-gather.9
  47.0 46.3 all-gather.5
  95.2 46.7 all-gather.13
  143.6 46.6 all-gather.11
  194.1 45.7 all-gather.7
  331.5 50.3 reduce-scatter.4
  384.4 44.8 reduce-scatter.10
  431.9 44.8 reduce-scatter.8
  479.4 44.8 reduce-scatter.6
where the time goes:
time: 536 us; the launch traced here: 535 us
  waiting for transfers between devices  399 us (74%)
  matrix products  50.7 us (9%)
  local copies, waits for them, and re-layouts  39.6 us (7%)
  starting transfers between devices  21.9 us (4%)
  between operations  14 us (3%)
  other arithmetic  9.62 us (2%)
    all_to_all x1, waiting for transfers between devices, per_device(): lax.all_to_all(pack(placing, full_z), 'expert', split_axis=0, concat_axis...  103 us
    all_to_all x1, waiting for transfers between devices, per_device(): lax.all_to_all(pack(placing_tok, full_tok), 'expert', split_axis=0, conca...  80.2 us
    reduce_scatter x1, waiting for transfers between devices, per_device(): lax.psum_scatter(part_up[None].astype(jnp.bfloat16), 'dp', scatter_dimens...  44.9 us
    reduce_scatter x1, waiting for transfers between devices, per_device(): lax.psum_scatter(part_gate[None].astype(jnp.bfloat16), 'dp', scatter_dime...  44.9 us
    reduce_scatter x1, waiting for transfers between devices, per_device(): lax.psum_scatter(part_down[None].astype(jnp.bfloat16), 'dp', scatter_dime...  37.2 us
    reduce_scatter x1, waiting for transfers between devices, per_device(): lax.psum_scatter(slot_partial.astype(jnp.bfloat16), 'ffn', scatter_dimens...  31.3 us
    all_gather x1, waiting for transfers between devices, per_device(): lax.all_gather(tokens, 'ffn', axis=1, tiled=True)  27.7 us
    all_gather x1, waiting for transfers between devices, per_device(): lax.all_gather(scaled, 'ffn', axis=1, tiled=True)  27.3 us
  transfers between devices with their start and end apart: 12, of which 8 were waited for; matrix products, arithmetic and copies ran while one was open for 16% of the time, Pallas kernels for 0%

commit v1 on v0

--- a/solution.py
+++ b/solution.py
@@ -37,7 +37,9 @@
 
     full_tok, full_z = (
         lax.all_gather(tokens, "ffn", axis=1, tiled=True),
-        lax.all_gather(scaled, "ffn", axis=1, tiled=True),
+        jnp.concatenate(
+            lax.all_to_all(jnp.stack([scaled] * lax.axis_size("ffn")), "ffn", 0, 0), axis=1
+        ),
     )
     recv_x, recv_z = (
         lax.all_to_all(

time: 536 us -> 572 us (1.067)
  waiting for transfers between devices: 399 us -> 423 us
  starting transfers between devices: 21.9 us -> 31 us
    all_to_all x1, waiting for transfers between devices: 80.2 us -> 108 us  [per_device(): lax.all_to_all(pack(placing_tok, full_tok), 'expert', split_axis=0, conca...]
    all_gather x1 -> x0, waiting for transfers between devices: 27.3 us -> none  [per_device(): lax.all_gather(scaled, 'ffn', axis=1, tiled=True)]
    all_to_all x1, waiting for transfers between devices: 103 us -> 113 us  [per_device(): lax.all_to_all(pack(placing, full_z), 'expert', split_axis=0, concat_axis...]
    all_gather x1, waiting for transfers between devices: 27.7 us -> 36 us  [per_device(): lax.all_gather(tokens, 'ffn', axis=1, tiled=True)]
    all_to_all x0 -> x1, waiting for transfers between devices: none -> 6.26 us  [per_device(): lax.all_to_all(jnp.stack([scaled] * lax.axis_size('ffn')), 'ffn', 0, 0)]
where the time goes in v1:
time: 572 us; the launch traced here: 571 us
  waiting for transfers between devices  423 us (74%)
  matrix products  50.2 us (9%)
  local copies, waits for them, and re-layouts  42.2 us (7%)
  starting transfers between devices  31 us (5%)
  between operations  15.6 us (3%)
  other arithmetic  8.69 us (2%)
    all_to_all x1, waiting for transfers between devices, per_device(): lax.all_to_all(pack(placing, full_z), 'expert', split_axis=0, concat_axis...  113 us
    all_to_all x1, waiting for transfers between devices, per_device(): lax.all_to_all(pack(placing_tok, full_tok), 'expert', split_axis=0, conca...  108 us
    reduce_scatter x1, waiting for transfers between devices, per_device(): lax.psum_scatter(part_up[None].astype(jnp.bfloat16), 'dp', scatter_dimens...  44.8 us
    reduce_scatter x1, waiting for transfers between devices, per_device(): lax.psum_scatter(part_gate[None].astype(jnp.bfloat16), 'dp', scatter_dime...  44.8 us
    reduce_scatter x1, waiting for transfers between devices, per_device(): lax.psum_scatter(part_down[None].astype(jnp.bfloat16), 'dp', scatter_dime...  37.2 us
    all_gather x1, waiting for transfers between devices, per_device(): lax.all_gather(tokens, 'ffn', axis=1, tiled=True)  36 us
    reduce_scatter x1, waiting for transfers between devices, per_device(): lax.psum_scatter(slot_partial.astype(jnp.bfloat16), 'ffn', scatter_dimens...  30.9 us
    reshape x2, local copies, waits for them, and re-layouts, pack(): return packed.reshape(groups, capacity, rows.shape[1])  14.6 us
  transfers between devices with their start and end apart: 12, of which 8 were waited for; matrix products, arithmetic and copies ran while one was open for 16% of the time, Pallas kernels for 0%

profile of v1, /device:TPU:1, one launch (start us, length us, event | category | flops | bytes accessed | tf_op | source)
XLA Modules:
  0.0 571.0 jit_solution(7887270232983557613)
XLA Ops:
  8.0 0.7 all-gather.7.cloned.1.call-update
  8.7 0.8 copy.40
  9.7 2.7 mul.66
  12.4 2.5 mul.67
  14.9 0.2 multiply_convert_fusion
  15.1 0.5 copy.41
  15.6 2.0 stack.3
  17.7 5.0 all-to-all-start
  23.1 0.6 reduce-window.6
  23.6 0.2 slice_reduce_fusion
  24.0 0.1 reduce_sum.33
  24.3 36.0 %all-gather.7.cloned.1.call-done = bf16[128,7168]{1,0:T(8,128)(2,1)} async-done(((bf16[128,1792]{1,0:T(8,128)(2,1)}), bf16[128,7168]{1,0:T(8,128)(2,1)}) %all-gather.7.cloned.1.call-update) | async-done | bytes 1835024 | tf_op jit(solution)/shard_map/all_gather | solution.py:39
  60.3 4.9 convolution_convert_fusion
  65.2 7.3 %reshape.113 = bf16[16,20,7168]{2,1,0:T(8,128)(2,1)} reshape(bf16[320,7168]{1,0:T(8,128)(2,1)} %convolution_convert_fusion) | data formatting | bytes 9175040 | tf_op jit(solution)/shard_map/reshape | solution.py:36
  72.5 6.3 %all-to-all-done = bf16[4,256,1792]{1,2,0:T(8,128)(2,1)} async-done(((bf16[4,256,1792]{1,2,0:T(8,128)(2,1)}), bf16[4,256,1792]{1,2,0:T(8,128)(2,1)}, u32[]{:S(2)}, u32[]{:S(2)}) %all-to-all-start) | async-done | bytes 3670048 | tf_op jit(solution)/shard_map/all_to_all | solution.py:41
  78.8 12.0 %all-to-all-start.2 = ((bf16[16,20,7168]{2,1,0:T(8,128)(2,1)}), bf16[16,20,7168]{2,1,0:T(8,128)(2,1)}, u32[]{:S(2)}, u32[]{:S(2)}) async-start(bf16[16,20,7168]{2,1,0:T(8,128)(2,1)} %reshape.113), calls=%async_computation.2 | async-start | bytes 11010048 | tf_op jit(solution)/shard_map/all_to_all | solution.py:45
  90.9 0.5 all-gather.11.cloned.1.call-update
  91.4 0.5 all-gather.9.cloned.1.call-update
  92.0 5.5 convolution_convert_fusion.1
  97.5 7.3 %reshape.111 = bf16[16,20,7168]{2,1,0:T(8,128)(2,1)} reshape(bf16[320,7168]{1,0:T(8,128)(2,1)} %convolution_convert_fusion.1) | data formatting | bytes 9175040 | tf_op jit(solution)/shard_map/reshape | solution.py:36
  104.8 107.6 %all-to-all-done.2 = bf16[16,20,7168]{2,1,0:T(8,128)(2,1)} async-done(((bf16[16,20,7168]{2,1,0:T(8,128)(2,1)}), bf16[16,20,7168]{2,1,0:T(8,128)(2,1)}, u32[]{:S(2)}, u32[]{:S(2)}) %all-to-all-start.2) | async-done | bytes 4587552 | tf_op jit(solution)/shard_map/all_to_all | solution.py:45
  212.4 5.5 all-to-all-start.1
  218.0 0.5 all-gather.5.cloned.1.call-update
  218.5 0.2 reduce-scatter.5.cloned.1.call-start
  218.7 7.3 %reshape.114 = bf16[320,7168]{1,0:T(8,128)(2,1)} reshape(bf16[16,20,7168]{2,1,0:T(8,128)(2,1)} %all-to-all-done.2) | data formatting | bytes 9175040 | tf_op jit(solution)/shard_map/reshape | solution.py:52
  226.1 113.5 %all-to-all-done.1 = bf16[16,20,7168]{2,1,0:T(8,128)(2,1)} async-done(((bf16[16,20,7168]{2,1,0:T(8,128)(2,1)}), bf16[16,20,7168]{2,1,0:T(8,128)(2,1)}, u32[]{:S(2)}, u32[]{:S(2)}) %all-to-all-start.1) | async-done | bytes 4587552 | tf_op jit(solution)/shard_map/all_to_all | solution.py:48
  339.5 7.3 %reshape.112 = bf16[320,7168]{1,0:T(8,128)(2,1)} reshape(bf16[16,20,7168]{2,1,0:T(8,128)(2,1)} %all-to-all-done.1) | data formatting | bytes 9175040 | tf_op jit(solution)/shard_map/reshape | solution.py:53
  346.9 4.8 fusion.6
  351.7 4.8 fusion.9
  356.5 5.0 multiply_convert_fusion.2
  361.5 1.4 fusion.4
  362.9 0.6 copy-done.1
  363.6 3.6 fusion
  367.2 6.3 %fusion.3 = bf16[1,256,7168]{2,1,0:T(8,128)(2,1)} fusion(bf16[320,7168]{1,0:T(8,128)(2,1)} %reshape.112, f32[320,256]{1,0:T(8,128)S(1)} %fusion.9, f32[320,256]{1,0:T(8,128)S(1)} %fusion.6), kind=kOutput, calls=%fused_computation.9 | convolution fusion | flops 1176731648 | bytes 8912896 | tf_op jit(solution)/shard_map/dot_general | solution.py:72
  373.5 6.3 %fusion.2 = bf16[1,7168,256]{2,1,0:T(8,128)(2,1)} fusion(bf16[320,7168]{1,0:T(8,128)(2,1)} %reshape.114, bf16[320,256]{1,0:T(8,128)(2,1)S(1)} %get-tuple-element.4), kind=kOutput, calls=%fused_computation.8 | convolution fusion | flops 1176240128 | bytes 8421376 | tf_op jit(solution)/shard_map/dot_general | solution.py:71
  379.8 0.3 reduce-scatter.7.cloned.1.call-start
  380.1 6.3 %fusion.1 = bf16[1,7168,256]{2,1,0:T(8,128)(2,1)} fusion(bf16[320,7168]{1,0:T(8,128)(2,1)} %reshape.114, bf16[320,256]{1,0:T(8,128)(2,1)S(1)} %get-tuple-element.5), kind=kOutput, calls=%fused_computation.7 | convolution fusion | flops 1176240128 | bytes 8421376 | tf_op jit(solution)/shard_map/dot_general | solution.py:68
  386.4 30.9 %reduce-scatter.5.cloned.1.call-done = bf16[320,1792]{1,0:T(8,128)(2,1)} async-done(((bf16[320,7168]{1,0:T(8,128)(2,1)}), bf16[320,1792]{1,0:T(8,128)(2,1)}) %reduce-scatter.5.cloned.1.call-update) | async-done | bytes 1146896 | tf_op jit(solution)/shard_map/reduce_scatter | solution.py:90
  417.3 2.3 reshape.115
  419.6 7.8 %all-to-all-start.3 = ((bf16[16,20,1792]{2,1,0:T(8,128)(2,1)}), bf16[16,20,1792]{2,1,0:T(8,128)(2,1)S(1)}, u32[]{:S(2)}, u32[]{:S(2)}) async-start(bf16[16,20,1792]{2,1,0:T(8,128)(2,1)} %reshape.115), calls=%async_computation.4 | async-start | bytes 2752512 | tf_op jit(solution)/shard_map/all_to_all | solution.py:94
  427.6 37.2 %reduce-scatter.11.cloned.1.call-done = bf16[1,256,1792]{2,1,0:T(8,128)(2,1)} async-done(((bf16[1,256,7168]{2,1,0:T(8,128)(2,1)}), bf16[1,256,1792]{2,1,0:T(8,128)(2,1)}) %reduce-scatter.11.cloned.1.call-update) | async-done | bytes 917520 | tf_op jit(solution)/shard_map/reduce_scatter | solution.py:80
  464.8 2.5 convert_element_type.90
  467.3 44.8 %reduce-scatter.9.cloned.1.call-done = bf16[1,1792,256]{2,1,0:T(8,128)(2,1)} async-done(((bf16[1,7168,256]{2,1,0:T(8,128)(2,1)}), bf16[1,1792,256]{2,1,0:T(8,128)(2,1)}) %reduce-scatter.9.cloned.1.call-update) | async-done | bytes 917520 | tf_op jit(solution)/shard_map/reduce_scatter | solution.py:77
  512.1 2.5 convert_element_type.86
  514.7 44.8 %reduce-scatter.7.cloned.1.call-done = bf16[1,1792,256]{2,1,0:T(8,128)(2,1)} async-done(((bf16[1,7168,256]{2,1,0:T(8,128)(2,1)}), bf16[1,1792,256]{2,1,0:T(8,128)(2,1)}) %reduce-scatter.7.cloned.1.call-update) | async-done | bytes 917520 | tf_op jit(solution)/shard_map/reduce_scatter | solution.py:74
  559.4 2.5 convert_element_type.83
  562.0 0.3 reshape.117
  562.2 1.4 convolution_reduce_fusion
  (33 shorter events, 1.4 us)
Async XLA Ops:
  8.0 52.3 %all-gather.7.cloned.1.call-start = ((), (), s32[]{:S(2)}) async-start(), calls=%async_computation.9 | async-start | bytes 2293760 | tf_op jit(solution)/shard_map/all_gather | solution.py:39
  17.7 5.0 copy-start.2
  17.7 61.1 %all-to-all-start = ((bf16[4,256,1792]{1,2,0:T(8,128)(2,1)}), bf16[4,256,1792]{1,2,0:T(8,128)(2,1)}, u32[]{:S(2)}, u32[]{:S(2)}) async-start(bf16[4,256,1792]{1,2,0:T(8,128)(2,1)} %stack.3), calls=%async_computation | async-start | bytes 7340032 | tf_op jit(solution)/shard_map/all_to_all | solution.py:41
  78.8 133.6 %all-to-all-start.2 = ((bf16[16,20,7168]{2,1,0:T(8,128)(2,1)}), bf16[16,20,7168]{2,1,0:T(8,128)(2,1)}, u32[]{:S(2)}, u32[]{:S(2)}) async-start(bf16[16,20,7168]{2,1,0:T(8,128)(2,1)} %reshape.113), calls=%async_computation.2 | async-start | bytes 11010048 | tf_op jit(solution)/shard_map/all_to_all | solution.py:45
  90.8 256.1 %all-gather.11.cloned.1.call-start = ((), (), s32[]{:S(2)}) async-start(), calls=%async_computation.11 | async-start | bytes 4587520 | tf_op jit(solution)/shard_map/all_gather | solution.py:57
  91.4 260.3 %all-gather.9.cloned.1.call-start = ((), (), s32[]{:S(2)}) async-start(), calls=%async_computation.10 | async-start | bytes 4587520 | tf_op jit(solution)/shard_map/all_gather | solution.py:58
  212.4 127.1 %all-to-all-start.1 = ((bf16[16,20,7168]{2,1,0:T(8,128)(2,1)}), bf16[16,20,7168]{2,1,0:T(8,128)(2,1)}, u32[]{:S(2)}, u32[]{:S(2)}) async-start(bf16[16,20,7168]{2,1,0:T(8,128)(2,1)} %reshape.111), calls=%async_computation.1 | async-start | bytes 11010048 | tf_op jit(solution)/shard_map/all_to_all | solution.py:48
  217.9 138.6 %all-gather.5.cloned.1.call-start = ((), (), s32[]{:S(2)}) async-start(), calls=%async_computation.8 | async-start | bytes 4587520 | tf_op jit(solution)/shard_map/all_gather | solution.py:59
  218.5 198.8 %reduce-scatter.5.cloned.1.call-start = ((), (), s32[]{:S(2)}) async-start(), calls=%async_computation.12 | async-start | bytes 5734400 | tf_op jit(solution)/shard_map/reduce_scatter | solution.py:90
  356.5 5.0 copy-start
  361.5 2.0 copy-start.1
  367.1 97.6 %reduce-scatter.11.cloned.1.call-start = ((), (), s32[]{:S(2)}) async-start(), calls=%async_computation.15 | async-start | bytes 4587520 | tf_op jit(solution)/shard_map/reduce_scatter | solution.py:80
  373.5 138.6 %reduce-scatter.9.cloned.1.call-start = ((), (), s32[]{:S(2)}) async-start(), calls=%async_computation.14 | async-start | bytes 4587520 | tf_op jit(solution)/shard_map/reduce_scatter | solution.py:77
  379.8 179.6 %reduce-scatter.7.cloned.1.call-start = ((), (), s32[]{:S(2)}) async-start(), calls=%async_computation.13 | async-start | bytes 4587520 | tf_op jit(solution)/shard_map/reduce_scatter | solution.py:74
  419.6 142.4 %all-to-all-start.3 = ((bf16[16,20,1792]{2,1,0:T(8,128)(2,1)}), bf16[16,20,1792]{2,1,0:T(8,128)(2,1)S(1)}, u32[]{:S(2)}, u32[]{:S(2)}) async-start(bf16[16,20,1792]{2,1,0:T(8,128)(2,1)} %reshape.115), calls=%async_computation.4 | async-start | bytes 2752512 | tf_op jit(solution)/shard_map/all_to_all | solution.py:94
Sparse Core Ops, SparseCore 0:
  10.6 49.6 all-gather.6
  367.3 49.9 reduce-scatter.4
  419.8 44.8 reduce-scatter.10
  467.2 44.8 reduce-scatter.8
  514.5 44.8 reduce-scatter.6
Sparse Core Ops, SparseCore 1:
  93.1 45.2 all-gather.10
  140.1 46.5 all-gather.8
  220.2 45.2 all-gather.4
